TPU v7x, 128 devices: a whole 4x4x4 slice. The times are simulated.
128 devices in a mesh: front: 8 (over z, core), panel: 16 (over x, y).
Axes of the slice: x: 4, y: 4, z: 4, core: 2. Of those that a mesh axis runs over, the one named last changes fastest.
Arguments:
- pivot_columns: float32 [8, 8192, 1024], P('front', 'panel')
- child_rows: bfloat16 [8, 16, 16, 4, 8192], P('front', 'panel'), may hold values from -0.375 to 0.375
- slot_rows: int32 [8, 16, 16, 4], P('front', 'panel'), may hold values from -1 to 511, as said below
- parents: int32 [8], replicated, may hold values from 0 to 7, as said below
- pivot_rhs: float32 [8, 1024, 128], P('front'), may hold values from -6 to 6
- boundary_solution: float32 [8, 8192, 128], P('front', 'panel'), may hold values from -6 to 6
Outputs:
- panel_factor: float32 [8, 8192, 1024], P('front', 'panel')
- update_matrix: bfloat16 [8, 8192, 7168], P('front', 'panel')
- front_solution: float32 [8, 8192, 128], P('front', 'panel')
- child_solution: float32 [8, 16, 16, 4, 128], P('front', 'panel')
Inputs may be any that keep to these rules, and one draw needn't show every extreme that they name: parents[c] is the front of this level into which child front c's rows are added; a front may take several children or none. `slot_rows`: the live slots of each tile of 4 slots come first; the rows that one child front sends to one destination device are distinct; for each child front one destination device receives full tiles from every source device.
All inputs are finite; a program needn't handle non-finite values.
Results may differ from a plain program's by a relative error of at most 0.007.
Values may be sent and summed in bfloat16 or wider, within the bound.
A program may use at most 192 MiB of HBM per device.

v0:
```python
import jax
import jax.numpy as jnp
from jax import lax
from jax.sharding import PartitionSpec as P

K = 512
NSTEP = 2


def spread(shard, axis, root):
    mine = lax.axis_index(axis) == root
    return lax.psum(jnp.where(mine, shard, jnp.zeros_like(shard)), axis)


def outer_rows(mine, piece):
    return lax.dot_general(
        mine, piece, (((1,), (1,)), ((), ())), preferred_element_type=jnp.float32
    )


def scatter_term(slots, rows, local_ids, width):
    onehot = (slots.reshape(-1)[None, :] == local_ids[:, None]).astype(jnp.bfloat16)
    return jnp.dot(onehot, rows.reshape(-1, width), preferred_element_type=jnp.float32)


def on_device(pivot_columns, child_rows, slot_rows, parents, pivot_rhs, boundary_solution):
    highest = lax.Precision.HIGHEST
    panel_index = lax.axis_index("panel")
    front_index = lax.axis_index("front")
    piv_cols = pivot_columns[0]
    row_count = piv_cols.shape[0]
    pivots = piv_cols.shape[1]
    width = child_rows.shape[-1]
    rhs_count = pivot_rhs.shape[-1]
    local_ids = jnp.arange(row_count, dtype=jnp.int32)
    glob_rows = panel_index * row_count + local_ids
    rows_out = child_rows[0, 0]
    slots_out = slot_rows[0, 0]
    routed_rows, routed_slots = (
        lax.all_to_all(rows_out, "panel", split_axis=0, concat_axis=0, tiled=True),
        lax.all_to_all(slots_out, "panel", split_axis=0, concat_axis=0, tiled=True),
    )
    piece_rows = lax.all_gather(routed_rows[None], "front", axis=0, tiled=True)
    piece_slots = lax.all_gather(routed_slots[None], "front", axis=0, tiled=True)
    keeping = parents == front_index

    def add_rows(current):
        kept_slots = jnp.where(keeping[:, None, None], piece_slots, -1)
        return scatter_term(kept_slots, piece_rows, local_ids, width)

    def keep_same(current):
        return current

    assembled = lax.cond(
        jnp.any(keeping), add_rows, keep_same, jnp.zeros((row_count, width), jnp.float32)
    )
    work = assembled + jnp.concatenate(
        [piv_cols, jnp.zeros((row_count, width - pivots), jnp.float32)], axis=1
    )
    identity_block = jnp.eye(K, dtype=jnp.float32)

    def factor_block(values):
        lower = jnp.linalg.cholesky(values)
        return lax.linalg.triangular_solve(lower, identity_block, left_side=True, lower=True)

    def empty_block(values):
        return jnp.zeros_like(values)

    factors = []
    inverses = []
    for panel_step in range(NSTEP):
        low_edge = panel_step * K
        high_edge = low_edge + K
        root_rank = low_edge // row_count
        offset = low_edge - root_rank * row_count
        pivot_block = work[offset : offset + K, low_edge:high_edge]
        inverse = lax.cond(panel_index == root_rank, factor_block, empty_block, pivot_block)
        inverse = spread(inverse, "panel", root_rank)
        column = jnp.dot(work[:, low_edge:high_edge], inverse.T, precision=highest)
        column = jnp.where(glob_rows[:, None] >= low_edge, column, 0.0)
        packed = column.astype(jnp.bfloat16)
        factors.append(column)
        inverses.append(inverse)
        work = work - outer_rows(packed, lax.all_gather(packed, "panel", axis=0, tiled=True))
    factor_all = jnp.concatenate(factors, axis=1)
    trailing = work[:, pivots:]
    update_matrix = jnp.where(glob_rows[:, None] >= pivots, trailing, 0.0).astype(jnp.bfloat16)
    known = boundary_solution[0]
    right_side = pivot_rhs[0]

    def local_values(solved):
        extended = jnp.concatenate([solved, jnp.zeros((row_count, rhs_count), jnp.float32)], axis=0)
        begin = jnp.minimum(panel_index * row_count, pivots)
        segment = lax.dynamic_slice_in_dim(extended, begin, row_count)
        return jnp.where(glob_rows[:, None] < pivots, segment, known)

    solved = jnp.zeros((pivots, rhs_count), jnp.float32)
    contract_rows = (((0,), (0,)), ((), ()))
    for panel_step in reversed(range(NSTEP)):
        low_edge = panel_step * K
        high_edge = low_edge + K
        current = local_values(solved)
        masked = jnp.where(glob_rows[:, None] >= high_edge, factors[panel_step], 0.0)
        partial_sum = lax.dot_general(masked, current, contract_rows, precision=highest)
        carried = lax.psum(partial_sum, "panel")
        value = lax.dot_general(
            inverses[panel_step],
            right_side[low_edge:high_edge] - carried,
            contract_rows,
            precision=highest,
        )
        solved = solved.at[low_edge:high_edge].set(value)
    front_values = local_values(solved)
    slot_onehot = (routed_slots[..., None] == local_ids).astype(jnp.float32)
    piece = lax.all_gather(front_values[None], "front", axis=0, tiled=True)
    piece_count = piece.shape[0]
    weights = (jnp.arange(piece_count, dtype=jnp.int32) == parents[front_index]).astype(jnp.float32)
    chosen = jnp.einsum("n,nrh->rh", weights, piece, precision=highest)
    slot_values = jnp.einsum("psr,rh->psh", slot_onehot, chosen, precision=highest)
    child_values = lax.all_to_all(slot_values, "panel", split_axis=0, concat_axis=0, tiled=True)
    return (factor_all[None], update_matrix[None], front_values[None], child_values[None, None])


def solution(mesh):
    in_specs = (
        P("front", "panel", None),
        P("front", "panel", None, None, None),
        P("front", "panel", None, None),
        P(),
        P("front", None, None),
        P("front", "panel", None),
    )
    out_specs = (
        P("front", "panel", None),
        P("front", "panel", None),
        P("front", "panel", None),
        P("front", "panel", None, None, None),
    )
    return jax.shard_map(
        on_device, mesh=mesh, in_specs=in_specs, out_specs=out_specs, check_vma=False
    )
```

profile of v0, /device:TPU:0, one launch (start us, length us, event | category | flops | bytes accessed | tf_op | source)
XLA Modules:
  0.0 1002.9 jit_solution(4517287727802942974)
XLA Ops:
  7.2 24.1 %all_to_all.19 = bf16[16,4,8192]{2,1,0:T(4,128)(2,1)} all-to-all(bf16[16,4,8192]{2,1,0:T(4,128)(2,1)} %bitcast.145), channel_id=1, replica_groups=mesh['front'=8,'panel'=16] {'panel'}, dimensions={0} | all-to-all | bytes 2097152 | tf_op jit(solution)/shard_map/all_to_all | solution.py:40
  31.3 1.4 copy.30
  32.7 3.8 all-to-all-start
  38.6 5.4 all-to-all-done
  44.0 14.0 %all-gather = s32[128,1,4]{2,1,0:T(1,128)S(1)} all-gather(s32[16,1,4]{2,1,0:T(1,128)S(1)} %all-to-all-done), channel_id=2, replica_groups=mesh['front'=8,'panel'=16] {'front'}, dimensions={0}, use_global_device_ids=true | all-gather | bytes 2304 | tf_op jit(solution)/shard_map/all_gather | solution.py:44
  58.0 22.9 %all-gather.12.cloned.1.call-done = bf16[128,4,8192]{2,1,0:T(4,128)(2,1)} async-done(((bf16[16,4,8192]{2,1,0:T(4,128)(2,1)}), bf16[128,4,8192]{2,1,0:T(4,128)(2,1)}) %all-gather.12.cloned.1.call-update) | async-done | bytes 8388624 | tf_op jit(solution)/shard_map/all_gather | solution.py:43
  80.9 24.2 %conditional.3 = (f32[512,8192]{1,0:T(8,128)}) conditional(s32[]{:T(128)} %convert_element_type.26, () %tuple.36, (pred[8]{0:T(512)(128)(4,1)S(1)}, s32[8,16,4]{2,1,0:T(8,128)S(1)}, s32[512]{0:T(512)S(1)}, bf16[8,16,4,8192]{3,2,1,0:T(4,128)(2,1)}) %tuple.137), branch_computations={%region_1.0_spmd, %region_2.3_spmd} | conditional | flops 4295229952 | bytes 41955344 | solution.py:54
  81.0 12.5 %reshape.120 = bf16[512,8192]{1,0:T(8,128)(2,1)} reshape(bf16[8,16,4,8192]{3,2,1,0:T(4,128)(2,1)} %get-tuple-element.54) | data formatting | bytes 16777216 | tf_op jit(solution)/shard_map/cond/branch_1_fun/reshape | solution.py:23
  93.6 11.5 %fusion = f32[512,8192]{1,0:T(8,128)} fusion(bf16[512,8192]{1,0:T(8,128)(2,1)} %reshape.120, s32[512]{0:T(512)S(1)} %eq.3, s32[512]{0:T(512)S(1)} %get-tuple-element.53), kind=kOutput, calls=%fused_computation | convolution fusion | flops 4295229440 | bytes 25169920 | tf_op jit(solution)/shard_map/cond/branch_1_fun/dot_general | solution.py:23
  105.0 7.0 pad_add_fusion
  112.0 5.7 copy-done
  117.8 141.4 %conditional.4 = (f32[512,512]{0,1:T(8,128)}) conditional(s32[]{:T(128)} %convert_element_type.27, () %tuple.38, (f32[512,512]{1,0:T(8,128)S(1)}, f32[512,512]{1,0:T(8,128)S(1)}) %tuple.39), branch_computations={%region_3.4_spmd, %region_4.15_spmd} | conditional | flops 1412760064 | bytes 26743068 | solution.py:77
  119.7 11.7 %cholesky.286 = f32[128,128]{1,0:T(8,128)S(1)} custom-call(f32[128,128]{1,0:T(8,128)S(1)} %cholesky.426), custom_call_target="Cholesky" | custom-call | tf_op jit(solution)/shard_map/cond/branch_1_fun/jit(cholesky)/cholesky | solution.py:63
  131.4 9.8 custom-call.27
  143.9 11.7 %cholesky.305 = f32[128,128]{1,0:T(8,128)S(1)} custom-call(f32[128,128]{1,0:T(8,128)S(1)} %cholesky.430), custom_call_target="Cholesky" | custom-call | tf_op jit(solution)/shard_map/cond/branch_1_fun/jit(cholesky)/cholesky | solution.py:63
  157.7 10.0 %custom-call.28 = f32[1,128,128]{1,2,0:T(8,128)S(1)} custom-call(f32[1,128,128]{2,1,0:T(8,128)S(1)} %get-tuple-element.139), custom_call_target="InvertDiagBlocksLowerTriangular" | custom-call | tf_op jit(solution)/shard_map/cond/branch_1_fun/jit(cholesky)/cholesky | solution.py:63
  169.3 11.7 %cholesky.326 = f32[128,128]{1,0:T(8,128)S(1)} custom-call(f32[128,128]{1,0:T(8,128)S(1)} %cholesky.435), custom_call_target="Cholesky" | custom-call | tf_op jit(solution)/shard_map/cond/branch_1_fun/jit(cholesky)/cholesky | solution.py:63
  182.3 9.8 custom-call.29
  193.6 11.7 %cholesky.343 = f32[128,128]{1,0:T(8,128)S(1)} custom-call(f32[128,128]{1,0:T(8,128)S(1)} %convolution_subtract_fusion.5), custom_call_target="Cholesky" | custom-call | tf_op jit(solution)/shard_map/cond/branch_1_fun/jit(cholesky)/cholesky | solution.py:63
  207.2 8.0 while.6
  207.9 1.4 bitcast_dynamic-update-slice_fusion.5
  209.9 1.4 bitcast_dynamic-update-slice_fusion.5
  211.9 1.4 bitcast_dynamic-update-slice_fusion.5
  213.9 1.4 bitcast_dynamic-update-slice_fusion.5
  215.3 39.3 %custom-call.30 = f32[4,128,128]{1,2,0:T(8,128)S(1)} custom-call(f32[4,128,128]{2,1,0:T(8,128)S(1)} %get-tuple-element.77), custom_call_target="InvertDiagBlocksLowerTriangular" | custom-call | tf_op jit(solution)/shard_map/cond/branch_1_fun/triangular_solve/custom-call.3 | solution.py:64
  259.3 2.3 broadcast_select_fusion.2
  261.7 82.1 %all-reduce.11.cloned.1.call-done = f32[512,512]{0,1:T(8,128)} async-done(((f32[512,512]{0,1:T(8,128)}), f32[512,512]{0,1:T(8,128)}) %all-reduce.11.cloned.1.call-update) | async-done | bytes 1048592 | tf_op jit(solution)/shard_map/psum | solution.py:12
  343.8 4.2 fusion.110
  348.1 77.5 %all-gather.8.cloned.1.call-done = bf16[8192,512]{0,1:T(8,128)(2,1)} async-done(((bf16[512,512]{0,1:T(8,128)(2,1)}), bf16[8192,512]{0,1:T(8,128)(2,1)}) %all-gather.8.cloned.1.call-update) | async-done | bytes 8388624 | tf_op jit(solution)/shard_map/all_gather | solution.py:84
  425.6 18.7 %convolution_subtract_fusion.12 = f32[512,8192]{1,0:T(8,128)} fusion(f32[512,8192]{1,0:T(8,128)} %copy-done, bf16[512,512]{0,1:T(8,128)(2,1)} %get-tuple-element.163, bf16[8192,512]{0,1:T(8,128)(2,1)} %all-gather.8.cloned.1.call-done), kind=kOutput, calls=%fused_computation.141 | convolution fusion | flops 4299161600 | bytes 42467328 | tf_op jit(solution)/shard_map/dot_general | solution.py:16
  445.6 8.3 conditional.5
  455.1 237.6 %all-reduce.13.cloned.1.call-done = f32[512,512]{0,1:T(8,128)} async-done(((f32[512,512]{0,1:T(8,128)}), f32[512,512]{0,1:T(8,128)}) %all-reduce.13.cloned.1.call-update) | async-done | bytes 1048592 | tf_op jit(solution)/shard_map/psum | solution.py:12
  692.7 4.2 fusion.111
  697.0 1.8 fusion.69
  698.8 83.3 %all-reduce.15.cloned.1.call-done = f32[512,128]{1,0:T(8,128)} async-done(((f32[512,128]{1,0:T(8,128)}), f32[512,128]{1,0:T(8,128)}) %all-reduce.15.cloned.1.call-update) | async-done | bytes 262160 | tf_op jit(solution)/shard_map/psum | solution.py:105
  782.1 2.3 fusion.85
  784.4 1.8 fusion.71
  786.3 83.5 %all-reduce.17.cloned.1.call-done = f32[512,128]{1,0:T(8,128)} async-done(((f32[512,128]{1,0:T(8,128)}), f32[512,128]{1,0:T(8,128)}) %all-reduce.17.cloned.1.call-update) | async-done | bytes 262160 | tf_op jit(solution)/shard_map/psum | solution.py:105
  869.8 2.3 fusion.86
  874.5 23.5 %all-gather.14.cloned.1.call-done = f32[4096,128]{1,0:T(8,128)} async-done(((f32[512,128]{1,0:T(8,128)}), f32[4096,128]{1,0:T(8,128)}) %all-gather.14.cloned.1.call-update) | async-done | bytes 2097168 | tf_op jit(solution)/shard_map/all_gather | solution.py:115
  898.0 4.4 fusion.67
  903.3 7.1 all-to-all-start.2
  910.4 1.5 maximum_bitcast_fusion
  911.9 2.9 copy.37
  914.8 3.1 all-to-all-done.2
  918.0 60.9 %all-gather.10.cloned.1.call-done = bf16[8192,512]{0,1:T(8,128)(2,1)} async-done(((bf16[512,512]{0,1:T(8,128)(2,1)}), bf16[8192,512]{0,1:T(8,128)(2,1)}) %all-gather.10.cloned.1.call-update) | async-done | bytes 8388624 | tf_op jit(solution)/shard_map/all_gather | solution.py:84
  978.8 7.1 fusion.112
  986.0 9.0 fusion.66
  (88 shorter events, 26.3 us)
Async XLA Ops:
  7.2 73.7 %all-gather.12.cloned.1.call-start = ((), (), s32[]{:S(2)}) async-start(), calls=%async_computation.9 | async-start | bytes 9437184 | tf_op jit(solution)/shard_map/all_gather | solution.py:43
  32.7 11.3 %all-to-all-start = ((s32[16,1,4]{2,1,0:T(1,128)}), s32[16,1,4]{2,1,0:T(1,128)S(1)}, u32[]{:S(2)}, u32[]{:S(2)}) async-start(s32[16,1,4]{2,1,0:T(1,128)} %copy.30), calls=%async_computation | async-start | bytes 16384 | tf_op jit(solution)/shard_map/all_to_all | solution.py:41
  36.5 307.3 %all-reduce.11.cloned.1.call-start = ((), (), s32[]{:S(2)}) async-start(), calls=%async_computation.3 | async-start | bytes 2097152 | tf_op jit(solution)/shard_map/psum | solution.py:12
  112.0 5.7 copy-start
  118.7 1.0 copy-start.2
  261.6 164.0 %all-gather.8.cloned.1.call-start = ((), (), s32[]{:S(2)}) async-start(), calls=%async_computation.4 | async-start | bytes 8912896 | tf_op jit(solution)/shard_map/all_gather | solution.py:84
  348.0 344.7 %all-reduce.13.cloned.1.call-start = ((), (), s32[]{:S(2)}) async-start(), calls=%async_computation.5 | async-start | bytes 2097152 | tf_op jit(solution)/shard_map/psum | solution.py:12
  445.6 251.4 %copy-start.4 = (f32[1,512,128]{2,1,0:T(8,128)S(1)}, f32[1,512,128]{2,1,0:T(8,128)}, u32[]{:S(2)}) copy-start(f32[1,512,128]{2,1,0:T(8,128)} %param.24) | copy-start | bytes 786436
  453.8 328.3 %copy-start.6 = (f32[1,1024,128]{2,1,0:T(8,128)S(1)}, f32[1,1024,128]{2,1,0:T(8,128)}, u32[]{:S(2)}) copy-start(f32[1,1024,128]{2,1,0:T(8,128)} %param.23) | copy-start | bytes 1572868
  453.8 419.9 %copy-start.7 = (s32[8]{0:T(128)S(1)}, s32[8]{0:T(128)}, u32[]{:S(2)}) copy-start(s32[8]{0:T(128)} %param.22) | copy-start | bytes 100
  454.9 327.2 %all-reduce.15.cloned.1.call-start = ((), (), s32[]{:S(2)}) async-start(), calls=%async_computation.7 | async-start | bytes 524288 | tf_op jit(solution)/shard_map/psum | solution.py:105
  698.8 171.0 %all-reduce.17.cloned.1.call-start = ((), (), s32[]{:S(2)}) async-start(), calls=%async_computation.8 | async-start | bytes 524288 | tf_op jit(solution)/shard_map/psum | solution.py:105
  784.4 194.4 %copy-start.1 = (bf16[512,512]{0,1:T(8,128)(2,1)S(1)}, bf16[512,512]{0,1:T(8,128)(2,1)}, u32[]{:S(2)}) copy-start(bf16[512,512]{0,1:T(8,128)(2,1)} %get-tuple-element.165) | copy-start | bytes 1572868
  786.2 111.8 %all-gather.14.cloned.1.call-start = ((), (), s32[]{:S(2)}) async-start(), calls=%async_computation.10 | async-start | bytes 2359296 | tf_op jit(solution)/shard_map/all_gather | solution.py:115
  873.0 105.8 %all-gather.10.cloned.1.call-start = ((), (), s32[]{:S(2)}) async-start(), calls=%async_computation.6 | async-start | bytes 8912896 | tf_op jit(solution)/shard_map/all_gather | solution.py:84
  903.3 14.6 %all-to-all-start.2 = ((f32[16,4,128]{2,1,0:T(4,128)}), f32[16,4,128]{2,1,0:T(4,128)S(1)}, u32[]{:S(2)}, u32[]{:S(2)}) async-start(f32[16,4,128]{2,1,0:T(4,128)} %copy.36), calls=%async_computation.2 | async-start | bytes 65536 | tf_op jit(solution)/shard_map/all_to_all | solution.py:120
Sparse Core Ops, SparseCore 0:
  31.4 49.3 all-gather.11
  261.7 82.0 all-reduce.10
  348.1 77.4 all-gather.7
  455.1 237.5 all-reduce.12
  698.9 83.2 all-reduce.14
  786.3 83.3 all-reduce.16
  873.2 24.8 all-gather.13
  900.1 78.6 all-gather.9
where the time goes:
time: 1010 us; the launch traced here: 1000 us
  waiting for transfers between devices  681 us (67%)
  other arithmetic  142 us (14%)
  matrix products  67.1 us (7%)
  blocking collectives  38.1 us (4%)
  local copies, waits for them, and re-layouts  37.7 us (4%)
  between operations  15.5 us (2%)
  starting transfers between devices  11.3 us (1%)
  loops' own time  10.5 us (1%)
    psum x2, waiting for transfers between devices, spread(): return lax.psum(jnp.where(mine, shard, jnp.zeros_like(shard)), axis)  320 us
    psum x2, waiting for transfers between devices, on_device(): carried = lax.psum(partial_sum, 'panel')  167 us
    all_gather x2, waiting for transfers between devices, on_device(): lax.all_gather(packed, 'panel', axis=0, tiled=True)  138 us
    another operation x14, other arithmetic, factor_block(): lower = jnp.linalg.cholesky(values)  78.6 us
    another operation x5, other arithmetic, factor_block(): lax.linalg.triangular_solve(lower, identity_block, left_side=True, lower=...  40 us
    dot_general x2, matrix products, outer_rows(): lax.dot_general(mine, piece, (((1,), (1,)), ((), ())), preferred_element_...  25.8 us
    all_to_all x1, blocking collectives, on_device(): lax.all_to_all(rows_out, 'panel', split_axis=0, concat_axis=0, tiled=True)  24.1 us
    all_gather x1, waiting for transfers between devices, on_device(): piece = lax.all_gather(front_values[None], 'front', axis=0, tiled=True)  23.5 us
  transfers between devices with their start and end apart: 10, of which 10 were waited for; matrix products, arithmetic and copies ran while one was open for 1% of the time, Pallas kernels for 0%

commit v1 on v0

--- a/solution.py
+++ b/solution.py
@@ -102,7 +102,7 @@
         current = local_values(solved)
         masked = jnp.where(glob_rows[:, None] >= high_edge, factors[panel_step], 0.0)
         partial_sum = lax.dot_general(masked, current, contract_rows, precision=highest)
-        carried = lax.psum(partial_sum, "panel")
+        carried = jnp.sum(lax.all_gather(partial_sum, "panel"), axis=0)
         value = lax.dot_general(
             inverses[panel_step],
             right_side[low_edge:high_edge] - carried,

time: 1010 us -> 956 us (0.947)
  waiting for transfers between devices: 681 us -> 614 us
  other arithmetic: 142 us -> 153 us
    psum x2 -> x0, waiting for transfers between devices: 167 us -> none  [on_device(): carried = lax.psum(partial_sum, 'panel')]
    all_gather x0 -> x2, waiting for transfers between devices: none -> 101 us  [on_device(): carried = jnp.sum(lax.all_gather(partial_sum, 'panel'), axis=0)]
  transfers between devices with their start and end apart: 10 -> 10, of which waited for: 10 -> 9; matrix products, arithmetic and copies ran while one was open for 1% -> 4% of each run, Pallas kernels for 0% -> 0%
where the time goes in v1:
time: 956 us; the launch traced here: 950 us
  waiting for transfers between devices  614 us (64%)
  other arithmetic  153 us (16%)
  matrix products  72.4 us (8%)
  blocking collectives  38.1 us (4%)
  local copies, waits for them, and re-layouts  37.7 us (4%)
  between operations  15.5 us (2%)
  starting transfers between devices  11.3 us (1%)
    psum x2, waiting for transfers between devices, spread(): return lax.psum(jnp.where(mine, shard, jnp.zeros_like(shard)), axis)  322 us
    all_gather x2, waiting for transfers between devices, on_device(): lax.all_gather(packed, 'panel', axis=0, tiled=True)  146 us
    all_gather x2, waiting for transfers between devices, on_device(): carried = jnp.sum(lax.all_gather(partial_sum, 'panel'), axis=0)  101 us
    another operation x14, other arithmetic, factor_block(): lower = jnp.linalg.cholesky(values)  78.6 us
    another operation x5, other arithmetic, factor_block(): lax.linalg.triangular_solve(lower, identity_block, left_side=True, lower=...  40 us
    dot_general x2, matrix products, outer_rows(): lax.dot_general(mine, piece, (((1,), (1,)), ((), ())), preferred_element_...  30.3 us
    all_to_all x1, blocking collectives, on_device(): lax.all_to_all(rows_out, 'panel', split_axis=0, concat_axis=0, tiled=True)  24.1 us
    all_gather x1, waiting for transfers between devices, on_device(): piece_rows = lax.all_gather(routed_rows[None], 'front', axis=0, tiled=True)  22.9 us
  transfers between devices with their start and end apart: 10, of which 9 were waited for; matrix products, arithmetic and copies ran while one was open for 4% of the time, Pallas kernels for 0%

profile of v1, /device:TPU:0, one launch (start us, length us, event | category | flops | bytes accessed | tf_op | source)
XLA Modules:
  0.0 949.5 jit_solution(5342520572423745340)
XLA Ops:
  7.2 24.1 %all_to_all.19 = bf16[16,4,8192]{2,1,0:T(4,128)(2,1)} all-to-all(bf16[16,4,8192]{2,1,0:T(4,128)(2,1)} %bitcast.149), channel_id=1, replica_groups=mesh['front'=8,'panel'=16] {'panel'}, dimensions={0} | all-to-all | bytes 2097152 | tf_op jit(solution)/shard_map/all_to_all | solution.py:40
  32.7 3.8 all-to-all-start
  38.6 5.4 all-to-all-done
  44.0 14.0 %all-gather = s32[128,1,4]{2,1,0:T(1,128)S(1)} all-gather(s32[16,1,4]{2,1,0:T(1,128)S(1)} %all-to-all-done), channel_id=2, replica_groups=mesh['front'=8,'panel'=16] {'front'}, dimensions={0}, use_global_device_ids=true | all-gather | bytes 2304 | tf_op jit(solution)/shard_map/all_gather | solution.py:44
  58.0 22.9 %all-gather.16.cloned.1.call-done = bf16[128,4,8192]{2,1,0:T(4,128)(2,1)} async-done(((bf16[16,4,8192]{2,1,0:T(4,128)(2,1)}), bf16[128,4,8192]{2,1,0:T(4,128)(2,1)}) %all-gather.16.cloned.1.call-update) | async-done | bytes 8388624 | tf_op jit(solution)/shard_map/all_gather | solution.py:43
  80.9 24.2 %conditional.3 = (f32[512,8192]{1,0:T(8,128)}) conditional(s32[]{:T(128)} %convert_element_type.26, () %tuple.36, (pred[8]{0:T(512)(128)(4,1)S(1)}, s32[8,16,4]{2,1,0:T(8,128)S(1)}, s32[512]{0:T(512)S(1)}, bf16[8,16,4,8192]{3,2,1,0:T(4,128)(2,1)}) %tuple.137), branch_computations={%region_1.0_spmd, %region_2.3_spmd} | conditional | flops 4295229952 | bytes 41955344 | solution.py:54
  81.0 12.5 %reshape.120 = bf16[512,8192]{1,0:T(8,128)(2,1)} reshape(bf16[8,16,4,8192]{3,2,1,0:T(4,128)(2,1)} %get-tuple-element.54) | data formatting | bytes 16777216 | tf_op jit(solution)/shard_map/cond/branch_1_fun/reshape | solution.py:23
  93.6 11.5 %fusion = f32[512,8192]{1,0:T(8,128)} fusion(bf16[512,8192]{1,0:T(8,128)(2,1)} %reshape.120, s32[512]{0:T(512)S(1)} %eq.3, s32[512]{0:T(512)S(1)} %get-tuple-element.53), kind=kOutput, calls=%fused_computation | convolution fusion | flops 4295229440 | bytes 25169920 | tf_op jit(solution)/shard_map/cond/branch_1_fun/dot_general | solution.py:23
  105.0 7.0 pad_add_fusion
  112.0 5.7 copy-done
  117.8 141.4 %conditional.4 = (f32[512,512]{0,1:T(8,128)}) conditional(s32[]{:T(128)} %convert_element_type.27, () %tuple.38, (f32[512,512]{1,0:T(8,128)S(1)}, f32[512,512]{1,0:T(8,128)S(1)}) %tuple.39), branch_computations={%region_3.4_spmd, %region_4.15_spmd} | conditional | flops 1412760064 | bytes 26743068 | solution.py:77
  119.7 11.7 %cholesky.286 = f32[128,128]{1,0:T(8,128)S(1)} custom-call(f32[128,128]{1,0:T(8,128)S(1)} %cholesky.426), custom_call_target="Cholesky" | custom-call | tf_op jit(solution)/shard_map/cond/branch_1_fun/jit(cholesky)/cholesky | solution.py:63
  131.4 9.8 %custom-call.27 = f32[1,128,128]{1,2,0:T(8,128)S(1)} custom-call(f32[1,128,128]{2,1,0:T(8,128)S(1)} %get-tuple-element.142), custom_call_target="InvertDiagBlocksLowerTriangular" | custom-call | tf_op jit(solution)/shard_map/cond/branch_1_fun/jit(cholesky)/cholesky | solution.py:63
  143.9 11.7 %cholesky.305 = f32[128,128]{1,0:T(8,128)S(1)} custom-call(f32[128,128]{1,0:T(8,128)S(1)} %cholesky.430), custom_call_target="Cholesky" | custom-call | tf_op jit(solution)/shard_map/cond/branch_1_fun/jit(cholesky)/cholesky | solution.py:63
  157.7 10.0 %custom-call.28 = f32[1,128,128]{1,2,0:T(8,128)S(1)} custom-call(f32[1,128,128]{2,1,0:T(8,128)S(1)} %get-tuple-element.139), custom_call_target="InvertDiagBlocksLowerTriangular" | custom-call | tf_op jit(solution)/shard_map/cond/branch_1_fun/jit(cholesky)/cholesky | solution.py:63
  169.3 11.7 %cholesky.326 = f32[128,128]{1,0:T(8,128)S(1)} custom-call(f32[128,128]{1,0:T(8,128)S(1)} %cholesky.435), custom_call_target="Cholesky" | custom-call | tf_op jit(solution)/shard_map/cond/branch_1_fun/jit(cholesky)/cholesky | solution.py:63
  182.3 9.8 %custom-call.29 = f32[1,128,128]{1,2,0:T(8,128)S(1)} custom-call(f32[1,128,128]{2,1,0:T(8,128)S(1)} %get-tuple-element.136), custom_call_target="InvertDiagBlocksLowerTriangular" | custom-call | tf_op jit(solution)/shard_map/cond/branch_1_fun/jit(cholesky)/cholesky | solution.py:63
  193.6 11.7 %cholesky.343 = f32[128,128]{1,0:T(8,128)S(1)} custom-call(f32[128,128]{1,0:T(8,128)S(1)} %convolution_subtract_fusion.5), custom_call_target="Cholesky" | custom-call | tf_op jit(solution)/shard_map/cond/branch_1_fun/jit(cholesky)/cholesky | solution.py:63
  207.2 8.0 while.6
  207.9 1.4 bitcast_dynamic-update-slice_fusion.5
  209.9 1.4 bitcast_dynamic-update-slice_fusion.5
  211.9 1.4 bitcast_dynamic-update-slice_fusion.5
  215.3 39.3 %custom-call.30 = f32[4,128,128]{1,2,0:T(8,128)S(1)} custom-call(f32[4,128,128]{2,1,0:T(8,128)S(1)} %get-tuple-element.77), custom_call_target="InvertDiagBlocksLowerTriangular" | custom-call | tf_op jit(solution)/shard_map/cond/branch_1_fun/triangular_solve/custom-call.3 | solution.py:64
  259.3 2.3 broadcast_select_fusion.2
  261.7 82.1 %all-reduce.9.cloned.1.call-done = f32[512,512]{0,1:T(8,128)} async-done(((f32[512,512]{0,1:T(8,128)}), f32[512,512]{0,1:T(8,128)}) %all-reduce.9.cloned.1.call-update) | async-done | bytes 1048592 | tf_op jit(solution)/shard_map/psum | solution.py:12
  343.8 4.2 fusion.110
  348.1 77.5 %all-gather.12.cloned.1.call-done = bf16[8192,512]{0,1:T(8,128)(2,1)} async-done(((bf16[512,512]{0,1:T(8,128)(2,1)}), bf16[8192,512]{0,1:T(8,128)(2,1)}) %all-gather.12.cloned.1.call-update) | async-done | bytes 8388624 | tf_op jit(solution)/shard_map/all_gather | solution.py:84
  425.6 18.7 %convolution_subtract_fusion.12 = f32[512,8192]{1,0:T(8,128)} fusion(f32[512,8192]{1,0:T(8,128)} %copy-done, bf16[512,512]{0,1:T(8,128)(2,1)} %get-tuple-element.163, bf16[8192,512]{0,1:T(8,128)(2,1)} %all-gather.12.cloned.1.call-done), kind=kOutput, calls=%fused_computation.141 | convolution fusion | flops 4299161600 | bytes 42467328 | tf_op jit(solution)/shard_map/dot_general | solution.py:16
  445.6 5.8 conditional.5
  452.6 240.2 %all-reduce.11.cloned.1.call-done = f32[512,512]{0,1:T(8,128)} async-done(((f32[512,512]{0,1:T(8,128)}), f32[512,512]{0,1:T(8,128)}) %all-reduce.11.cloned.1.call-update) | async-done | bytes 1048592 | tf_op jit(solution)/shard_map/psum | solution.py:12
  692.9 4.3 fusion.111
  697.2 1.8 fusion.69
  699.1 50.7 %all-gather.18.cloned.1.call-done = f32[8192,128]{1,0:T(8,128)} async-done(((f32[512,128]{1,0:T(8,128)}), f32[8192,128]{1,0:T(8,128)}) %all-gather.18.cloned.1.call-update) | async-done | bytes 4194320 | tf_op jit(solution)/shard_map/all_gather | solution.py:105
  749.8 3.1 reduce_sum.18
  752.9 2.0 fusion.85
  754.9 2.7 fusion.71
  758.7 50.2 %all-gather.20.cloned.1.call-done = f32[8192,128]{1,0:T(8,128)} async-done(((f32[512,128]{1,0:T(8,128)}), f32[8192,128]{1,0:T(8,128)}) %all-gather.20.cloned.1.call-update) | async-done | bytes 4194320 | tf_op jit(solution)/shard_map/all_gather | solution.py:105
  808.9 2.4 reduce_sum.19
  811.3 2.3 fusion.86
  813.6 1.9 fusion.82
  816.2 1.5 maximum_bitcast_fusion
  817.6 2.9 copy.37
  820.5 68.5 %all-gather.14.cloned.1.call-done = bf16[8192,512]{0,1:T(8,128)(2,1)} async-done(((bf16[512,512]{0,1:T(8,128)(2,1)}), bf16[8192,512]{0,1:T(8,128)(2,1)}) %all-gather.14.cloned.1.call-update) | async-done | bytes 8388624 | tf_op jit(solution)/shard_map/all_gather | solution.py:84
  889.0 11.7 %fusion.112 = f32[512,8192]{1,0:T(8,128)} fusion(bf16[512,512]{0,1:T(8,128)(2,1)S(1)} %copy-done.1, bf16[8192,512]{0,1:T(8,128)(2,1)} %all-gather.14.cloned.1.call-done), kind=kOutput, calls=%fused_computation.204 | convolution fusion | flops 4294967296 | bytes 25690112 | tf_op jit(solution)/shard_map/dot_general | solution.py:16
  900.7 15.5 %all-gather.22.cloned.1.call-done = f32[4096,128]{1,0:T(8,128)} async-done(((f32[512,128]{1,0:T(8,128)}), f32[4096,128]{1,0:T(8,128)}) %all-gather.22.cloned.1.call-update) | async-done | bytes 2097168 | tf_op jit(solution)/shard_map/all_gather | solution.py:115
  916.1 4.4 fusion.67
  921.4 6.8 all-to-all-start.2
  928.3 13.3 %fusion.66 = bf16[1,512,7168]{2,1,0:T(8,128)(2,1)} fusion(f32[512,8192]{1,0:T(8,128)} %fusion.112, f32[512,8192]{1,0:T(8,128)} %convolution_subtract_fusion.12, pred[512]{0:T(512)(128)(4,1)S(1)} %fusion.95), kind=kLoop, calls=%fused_computation.142 | loop fusion | flops 11010048 | bytes 36700672 | tf_op jit(solution)/shard_map/broadcast_in_dim | solution.py:121
  (90 shorter events, 28.4 us)
Async XLA Ops:
  7.2 73.7 %all-gather.16.cloned.1.call-start = ((), (), s32[]{:S(2)}) async-start(), calls=%async_computation.7 | async-start | bytes 9437184 | tf_op jit(solution)/shard_map/all_gather | solution.py:43
  32.7 11.3 %all-to-all-start = ((s32[16,1,4]{2,1,0:T(1,128)}), s32[16,1,4]{2,1,0:T(1,128)S(1)}, u32[]{:S(2)}, u32[]{:S(2)}) async-start(s32[16,1,4]{2,1,0:T(1,128)} %copy.30), calls=%async_computation | async-start | bytes 16384 | tf_op jit(solution)/shard_map/all_to_all | solution.py:41
  36.5 307.3 %all-reduce.9.cloned.1.call-start = ((), (), s32[]{:S(2)}) async-start(), calls=%async_computation.3 | async-start | bytes 2097152 | tf_op jit(solution)/shard_map/psum | solution.py:12
  112.0 5.7 copy-start
  118.7 1.0 copy-start.3
  261.6 164.0 %all-gather.12.cloned.1.call-start = ((), (), s32[]{:S(2)}) async-start(), calls=%async_computation.4 | async-start | bytes 8912896 | tf_op jit(solution)/shard_map/all_gather | solution.py:84
  348.0 344.9 %all-reduce.11.cloned.1.call-start = ((), (), s32[]{:S(2)}) async-start(), calls=%async_computation.5 | async-start | bytes 2097152 | tf_op jit(solution)/shard_map/psum | solution.py:12
  445.6 251.6 %copy-start.5 = (f32[1,512,128]{2,1,0:T(8,128)S(1)}, f32[1,512,128]{2,1,0:T(8,128)}, u32[]{:S(2)}) copy-start(f32[1,512,128]{2,1,0:T(8,128)} %param.24) | copy-start | bytes 786436
  452.5 297.3 %all-gather.18.cloned.1.call-start = ((), (), s32[]{:S(2)}) async-start(), calls=%async_computation.8 | async-start | bytes 4456448 | tf_op jit(solution)/shard_map/all_gather | solution.py:105
  692.9 60.0 %copy-start.2 = (f32[512,512]{0,1:T(8,128)S(1)}, f32[512,512]{0,1:T(8,128)}, u32[]{:S(2)}) copy-start(f32[512,512]{0,1:T(8,128)} %all-reduce.11.cloned.1.call-done) | copy-start | bytes 3145732
  699.0 116.5 %copy-start.7 = (s32[8]{0:T(128)S(1)}, s32[8]{0:T(128)}, u32[]{:S(2)}) copy-start(s32[8]{0:T(128)} %param.22) | copy-start | bytes 100
  699.0 109.9 %all-gather.20.cloned.1.call-start = ((), (), s32[]{:S(2)}) async-start(), calls=%async_computation.9 | async-start | bytes 4456448 | tf_op jit(solution)/shard_map/all_gather | solution.py:105
  757.6 131.4 %copy-start.1 = (bf16[512,512]{0,1:T(8,128)(2,1)S(1)}, bf16[512,512]{0,1:T(8,128)(2,1)}, u32[]{:S(2)}) copy-start(bf16[512,512]{0,1:T(8,128)(2,1)} %get-tuple-element.165) | copy-start | bytes 1572868
  757.7 131.3 %all-gather.14.cloned.1.call-start = ((), (), s32[]{:S(2)}) async-start(), calls=%async_computation.6 | async-start | bytes 8912896 | tf_op jit(solution)/shard_map/all_gather | solution.py:84
  758.4 157.7 %all-gather.22.cloned.1.call-start = ((), (), s32[]{:S(2)}) async-start(), calls=%async_computation.10 | async-start | bytes 2359296 | tf_op jit(solution)/shard_map/all_gather | solution.py:115
  921.4 20.2 %all-to-all-start.2 = ((f32[16,4,128]{2,1,0:T(4,128)}), f32[16,4,128]{2,1,0:T(4,128)S(1)}, u32[]{:S(2)}, u32[]{:S(2)}) async-start(f32[16,4,128]{2,1,0:T(4,128)} %copy.36), calls=%async_computation.2 | async-start | bytes 65536 | tf_op jit(solution)/shard_map/all_to_all | solution.py:120
Sparse Core Ops, SparseCore 0:
  31.4 49.3 all-gather.15
  261.7 82.0 all-reduce.8
  348.1 77.4 all-gather.11
  452.6 240.2 all-reduce.10
  699.1 50.6 all-gather.17
  757.8 51.0 all-gather.19
  811.0 77.9 all-gather.13
  891.3 24.7 all-gather.21
